TPU v7x, 256 devices: a whole 4x4x8 slice. The times are simulated.
256 devices in a mesh: dp: 4 (over x), rad: 8 (over y, z_lo), azi: 8 (over z_hi, core).
Axes of the slice: x: 4, y: 4, z: 8 (z_hi: 4, z_lo: 2; z = z_hi * 2 + z_lo), core: 2. Of those that a mesh axis runs over, the one named last changes fastest.
Arguments:
- inputs: bfloat16 [4, 96, 32, 64, 256], P('dp', None, 'rad', 'azi'), may hold values from -6 to 6
- weight: bfloat16 [96, 2592], P('dp'), may hold values from -0.125 to 0.125
- bias: bfloat16 [96], P('dp'), may hold values from -3 to 3
- cotangent: bfloat16 [4, 96, 32, 64, 256], P('dp', None, 'rad', 'azi'), may hold values from -6 to 6
Outputs:
- output: bfloat16 [4, 96, 32, 64, 256], P('dp', None, 'rad', 'azi')
- input_grad: bfloat16 [4, 96, 32, 64, 256], P('dp', None, 'rad', 'azi')
- weight_grad: float32 [96, 2592], P('dp')
- bias_grad: float32 [96], P('dp')
All inputs are finite; a program needn't handle non-finite values.
Results may differ from a plain program's by a relative error of at most 0.015.
Values may be sent and summed in bfloat16 or wider, within the bound.
No kernel may reach another device: no remote copies, remote signals or barrier semaphores. Data moves between devices by JAX's collectives and lax.ppermute only.
A program may use at most 128 MiB of HBM per device.

v0:
```python
import jax
import jax.numpy as jnp
from jax import lax
from jax.sharding import PartitionSpec as P

inverse_scale = 1.0 / 1024.0


def with_halo(cells, sides, width):
    for axis, dim in sides:
        count = lax.axis_size(axis)
        head = lax.slice_in_dim(cells, 0, width, axis=dim)
        tail = lax.slice_in_dim(cells, cells.shape[dim] - width, cells.shape[dim], axis=dim)
        cells = jnp.concatenate(
            [
                lax.ppermute(tail, axis, [(i, (i + 1) % count) for i in range(count)]),
                cells,
                lax.ppermute(head, axis, [((i + 1) % count, i) for i in range(count)]),
            ],
            axis=dim,
        )
    return cells


def rim_fix(extended):
    rad_index = lax.axis_index("rad")
    rad_last = lax.axis_size("rad") - 1
    low_rim = jnp.where(rad_index > 0, extended[:, :, :1], jnp.zeros_like(extended[:, :, :1]))
    high_rim = jnp.where(
        rad_index < rad_last, extended[:, :, -1:], jnp.zeros_like(extended[:, :, -1:])
    )
    return jnp.concatenate([low_rim, extended[:, :, 1:-1], high_rim], axis=2)


def axial_pad(extended):
    return jnp.pad(extended, ((0, 0), (0, 0), (0, 0), (0, 0), (1, 1)))


def extend_input(field):
    extended = rim_fix(with_halo(field, (("rad", 2), ("azi", 3)), 1))
    return axial_pad(extended)


def extend_grad(field):
    extended = rim_fix(with_halo(field, (("rad", 2), ("azi", 3)), 1))
    return axial_pad(extended)


def convolve(left, right, numbers):
    return lax.conv_general_dilated(
        left,
        right,
        (1, 1, 1),
        "VALID",
        dimension_numbers=numbers,
        preferred_element_type=jnp.float32,
    )


def on_device(inputs, weight, bias, cotangent):
    channels = inputs.shape[1]
    full_weight, full_bias = (
        lax.all_gather(weight, "dp", axis=0, tiled=True),
        lax.all_gather(bias, "dp", axis=0, tiled=True),
    )
    out_rows = full_weight.shape[0]
    kernel_taps = full_weight.reshape(out_rows, 3, 3, 3, channels)
    kernel_fwd = kernel_taps.transpose(0, 4, 1, 2, 3)
    kernel_back = kernel_taps[:, ::-1, ::-1, ::-1, :].transpose(4, 0, 1, 2, 3)
    padded = extend_input(inputs)
    preact = convolve(padded, kernel_fwd, ("NCDHW", "OIDHW", "NCDHW"))
    preact = preact + full_bias.astype(jnp.float32)[None, :, None, None, None]
    gate_value = jax.nn.sigmoid(preact)
    output = (preact * gate_value).astype(jnp.bfloat16)
    delta_z = (
        cotangent.astype(jnp.float32) * gate_value * (1.0 + preact * (1.0 - gate_value))
    ).astype(jnp.bfloat16)
    delta_pad = extend_grad(delta_z)
    backward = convolve(delta_pad, kernel_back, ("NCDHW", "OIDHW", "NCDHW"))
    kernel_grad = convolve(padded, delta_z, ("CNDHW", "IODHW", "NCDHW"))
    weight_term = (
        kernel_grad.transpose(1, 2, 3, 4, 0).reshape(out_rows, 27 * channels) * inverse_scale
    )
    bias_term = jnp.sum(delta_z.astype(jnp.float32), axis=(0, 2, 3, 4)) * inverse_scale
    group_part = (
        lax.psum_scatter(
            weight_term.astype(jnp.bfloat16), "dp", scatter_dimension=0, tiled=True
        ).astype(jnp.float32),
        lax.psum_scatter(
            bias_term.astype(jnp.bfloat16), "dp", scatter_dimension=0, tiled=True
        ).astype(jnp.float32),
    )
    weight_grad, bias_grad = lax.psum((group_part[0], group_part[1]), ("rad", "azi"))
    return (output, backward.astype(jnp.bfloat16), weight_grad, bias_grad)


def solution(mesh):
    return jax.shard_map(
        on_device,
        mesh=mesh,
        in_specs=(
            P("dp", None, "rad", "azi", None),
            P("dp", None),
            P("dp"),
            P("dp", None, "rad", "azi", None),
        ),
        out_specs=(
            P("dp", None, "rad", "azi", None),
            P("dp", None, "rad", "azi", None),
            P("dp", None),
            P("dp"),
        ),
        check_vma=False,
    )
```

profile of v0, /device:TPU:2, one launch (start us, length us, event | category | flops | bytes accessed | tf_op | source)
XLA Modules:
  0.0 530.9 jit_solution(4180190173391444999)
XLA Ops:
  7.2 1.2 fusion.42
  8.4 4.4 collective-permute-start.1
  12.8 9.5 %collective-permute-done.1 = bf16[1,96,1,8,256]{4,3,2,1,0:T(8,128)(2,1)S(1)} collective-permute-done((bf16[1,96,1,8,256]{4,3,2,1,0:T(8,128)(2,1)S(1)}, bf16[1,96,1,8,256]{4,3,2,1,0:T(8,128)(2,1)S(1)}, u32[]{:S(2)}, u32[]{:S(2)}) %collective-permute-start.1) | collective-permute-done | bytes 393248 | tf_op jit(solution)/shard_map/ppermute | solution.py:18
  22.3 8.0 %collective-permute-done = bf16[1,96,1,8,256]{4,3,2,1,0:T(8,128)(2,1)S(1)} collective-permute-done((bf16[1,96,1,8,256]{4,3,2,1,0:T(8,128)(2,1)S(1)}, bf16[1,96,1,8,256]{4,3,2,1,0:T(8,128)(2,1)S(1)}, u32[]{:S(2)}, u32[]{:S(2)}) %collective-permute-start) | collective-permute-done | bytes 393248 | tf_op jit(solution)/shard_map/ppermute | solution.py:16
  30.4 1.7 pad_maximum_fusion.3
  32.1 0.8 fusion.40
  32.9 0.8 copy.97
  33.6 0.6 fusion.43
  34.9 0.2 dynamic-update-slice
  35.1 8.6 %all-reduce = bf16[96]{0:T(256)(128)(2,1)S(1)} all-reduce(bf16[96]{0:T(256)(128)(2,1)S(1)} %dynamic-update-slice), channel_id=1, replica_groups=mesh['dp'=4,'rad'=8,'azi'=8] {'dp'}, use_global_device_ids=true, to_apply=%add | all-reduce | flops 96 | bytes 384
  43.8 12.8 %all_gather.6 = bf16[96,2592]{1,0:T(8,128)(2,1)S(1)} all-gather(bf16[24,2592]{1,0:T(8,128)(2,1)} %param.5), channel_id=1, replica_groups=mesh['dp'=4,'rad'=8,'azi'=8] {'dp'}, dimensions={0}, use_global_device_ids=true | all-gather | bytes 622080 | tf_op jit(solution)/shard_map/all_gather | solution.py:63
  56.6 1.1 copy.67
  57.7 4.6 copy.69
  63.0 0.9 collective-permute-start.3
  63.9 1.0 constant_dynamic-update-slice_fusion.2
  64.9 0.8 constant_dynamic-update-slice_fusion.1
  65.7 5.6 %collective-permute-done.3 = bf16[1,96,6,1,256]{4,1,3,2,0:T(8,128)(2,1)S(1)} collective-permute-done((bf16[1,96,6,1,256]{4,1,3,2,0:T(8,128)(2,1)S(1)}, bf16[1,96,6,1,256]{4,1,3,2,0:T(8,128)(2,1)S(1)}, u32[]{:S(2)}, u32[]{:S(2)}) %collective-permute-start.3) | collective-permute-done | bytes 294944 | tf_op jit(solution)/shard_map/ppermute | solution.py:18
  71.3 0.1 slice.65
  71.5 0.1 slice_select_fusion.1
  71.5 1.8 pad_maximum_fusion.1
  73.4 3.6 copy.88
  77.0 5.5 %pad.3.clone = bf16[96,6,10,1,264]{0,4,2,1,3:T(8,128)(2,1)} pad(bf16[96,6,10,1,256]{0,4,2,1,3:T(8,128)(2,1)} %copy.88, bf16[]{:T(256)} %constant.6.clone.1), padding=0_0x0_0x0_0x0_0x1_7 | pad | bytes 5990402 | tf_op jit(solution)/shard_map/concatenate | solution.py:32
  82.5 7.2 %reshape.21 = bf16[96,6,10,1,8,33]{0,5,4,2,1,3:T(8,128)(2,1)} reshape(bf16[96,6,10,1,264]{0,4,2,1,3:T(8,128)(2,1)} %pad.3.clone) | data formatting | bytes 6082560 | tf_op jit(solution)/shard_map/conv_general_dilated | solution.py:50
  89.7 3.1 copy.66
  92.9 17.9 %add_divide_fusion = (f32[4,8,8,33,96]{4,2,3,1,0:T(8,128)S(1)}, bf16[4,8,8,33,96]{4,2,3,1,0:T(8,128)(2,1)}, f32[4,8,8,33,96]{4,2,3,1,0:T(8,128)S(1)}) fusion(f32[96]{0:T(128)S(1)} %convert_element_type.36, pred[8,33]{0,1:T(8,128)(4,1)S(1)} %copy-done.8, bf16[96,3,3,3,96]{0,4,3,2,1:T(8,128)(2,1)S(1)} %bitcast.55, ...), kind=kOutput, calls=%fused_computation.6 | convolution fusion | flops 4222052352 | bytes 11810952 | tf_op jit(solution)/shard_map/conv_general_dilated | solution.py:50
  110.9 0.8 copy.71
  111.6 0.8 copy.70
  112.4 0.8 copy-done.1
  113.2 1.6 convert_reduce_fusion
  114.8 0.1 fusion.41
  114.9 1.2 copy.73
  116.2 1.2 copy.72
  117.4 2.0 collective-permute-start.4
  119.4 16.3 %copy.83 = bf16[1,96,6,10,256]{1,0,4,3,2:T(2,128)(2,1)} copy(bf16[1,96,6,10,256]{4,1,3,2,0:T(8,128)(2,1)} %get-tuple-element.25) | data formatting | bytes 5898240 | tf_op jit(solution)/shard_map/concatenate | solution.py:32
  135.8 63.2 %fusion.28 = bf16[96,3,3,3,96]{0,4,3,2,1:T(8,128)(2,1)S(1)} fusion(bf16[1,96,6,10,256]{1,0,4,3,2:T(2,128)(2,1)} %copy.83, bf16[1,96,4,8,256]{1,3,4,2,0:T(8,128)(2,1)S(1)} %get-tuple-element.19), kind=kOutput, calls=%fused_computation.38 | convolution fusion | flops 4066744320 | bytes 5019648 | tf_op jit(solution)/shard_map/transpose | solution.py:82
  199.0 0.3 copy.68
  199.2 1.5 slice_bitcast_fusion.3
  200.7 4.6 copy.86
  205.4 1.1 copy.85
  206.4 1.5 copy.75
  208.0 1.5 copy.74
  209.5 0.7 pad_maximum_fusion
  210.3 1.6 copy-done
  211.9 1.2 fusion.39
  213.1 0.5 copy.77
  213.6 3.8 collective-permute-start.7
  217.4 0.5 copy.76
  217.9 0.1 collective-permute-start.6
  218.0 11.4 %all-reduce.2 = bf16[96]{0:T(256)(128)(2,1)S(1)} all-reduce(bf16[96]{0:T(256)(128)(2,1)S(1)} %multiply_convert_fusion.1), channel_id=3, replica_groups=mesh['dp'=4,'rad'=8,'azi'=8] {'dp'}, use_global_device_ids=true, to_apply=%region_3.4.clone | all-reduce | flops 96 | bytes 384
  229.4 0.1 dynamic-slice_convert_fusion
  229.5 3.7 copy.78
  233.3 0.4 pad_maximum_fusion.2
  233.6 0.1 slice.75
  233.8 0.1 maximum_select_fusion.1
  233.9 0.4 maximum_bitcast_fusion
  234.3 3.7 copy.89
  238.0 5.4 %pad.5.clone = bf16[96,6,10,1,264]{0,4,2,1,3:T(8,128)(2,1)} pad(bf16[96,6,10,1,256]{0,4,2,1,3:T(8,128)(2,1)} %copy.89, bf16[]{:T(256)} %constant.6.clone.1), padding=0_0x0_0x0_0x0_0x1_7 | pad | bytes 5990402 | tf_op jit(solution)/shard_map/concatenate | solution.py:32
  243.4 7.2 %reshape.28 = bf16[96,6,10,1,8,33]{0,5,4,2,1,3:T(8,128)(2,1)} reshape(bf16[96,6,10,1,264]{0,4,2,1,3:T(8,128)(2,1)} %pad.5.clone) | data formatting | bytes 6082560 | tf_op jit(solution)/shard_map/conv_general_dilated | solution.py:50
  250.7 3.1 copy.81
  253.9 15.8 %select_convert_fusion = bf16[4,8,8,33,96]{4,2,3,1,0:T(8,128)(2,1)S(1)} fusion(pred[8,33]{0,1:T(8,128)(4,1)S(1)} %copy-done.9, bf16[96,3,3,3,96]{0,4,3,2,1:T(8,128)(2,1)S(1)} %bitcast.56, bf16[96,6,10,1,7,2]{0,4,5,2,1,3:T(8,128)(2,1)S(1)} %slice.76, bf16[96,6,10,1,8,33]{0,4,5,2,1,3:T(8,128)(2,1)S(1)} %copy.81), kind=kOutput, calls=%fused_computation.3 | convolution fusion | flops 4215564288 | bytes 5322504 | tf_op jit(solution)/shard_map/conv_general_dilated | solution.py:50
  269.6 0.3 copy.82
  269.9 0.1 slice_bitcast_fusion.2
  270.1 3.0 copy.87
  273.1 250.6 %all-reduce.5 = (f32[24,2592]{1,0:T(8,128)}, f32[24]{0:T(128)}) all-reduce(bf16[24,2592]{1,0:T(8,128)(2,1)} %reduce-scatter.4.cloned.1.call-done, f32[24]{0:T(128)S(1)} %dynamic-slice_convert_fusion), channel_id=1, replica_groups=mesh['dp'=4,'rad'=8,'azi'=8] {'rad','azi'}, use_global_device_ids=true, to_apply=%region_1.2 | all-reduce | flops 62232 | bytes 373440 | tf_op jit(solution)/shard_map/psum | solution.py:93
  (36 shorter events, 0.3 us)
Async XLA Ops:
  7.2 265.9 %reduce-scatter.4.cloned.1.call-start = ((), (), s32[]{:S(2)}) async-start(), calls=%async_computation.1 | async-start | bytes 645120
  8.4 13.9 %collective-permute-start.1 = (bf16[1,96,1,8,256]{4,3,2,1,0:T(8,128)(2,1)S(1)}, bf16[1,96,1,8,256]{4,3,2,1,0:T(8,128)(2,1)S(1)}, u32[]{:S(2)}, u32[]{:S(2)}) collective-permute-start(bf16[1,96,1,8,256]{4,3,2,1,0:T(8,128)(2,1)S(1)} %get-tuple-element.36), channel_id=1, source_target_pairs={{8,0},{16,8},{24,16},{32,24},{40,32},{48,40},{56,48},{0,56},{9,1},... | collective-permute-start | bytes 1179656 | tf_op jit(solution)/shard_map/ppermute | solution.py:18
  12.8 20.8 %copy-start.5 = (u32[256]{0:T(256)S(1)}, u32[256]{0:T(256)}, u32[]{:S(2)}) copy-start(u32[256]{0:T(256)} %constant.33) | copy-start | bytes 3076
  12.8 22.0 %copy-start.7 = (bf16[24]{0:T(256)(128)(2,1)S(1)}, bf16[24]{0:T(256)(128)(2,1)}, u32[]{:S(2)}) copy-start(bf16[24]{0:T(256)(128)(2,1)} %param.6) | copy-start | bytes 148
  12.8 17.5 %collective-permute-start = (bf16[1,96,1,8,256]{4,3,2,1,0:T(8,128)(2,1)S(1)}, bf16[1,96,1,8,256]{4,3,2,1,0:T(8,128)(2,1)S(1)}, u32[]{:S(2)}, u32[]{:S(2)}) collective-permute-start(bf16[1,96,1,8,256]{4,3,2,1,0:T(8,128)(2,1)S(1)} %get-tuple-element.35), channel_id=1, source_target_pairs={{0,8},{8,16},{16,24},{24,32},{32,40},{40,48},{48,56},{56,0},{1,9},... | collective-permute-start | bytes 1179656 | tf_op jit(solution)/shard_map/ppermute | solution.py:16
  33.6 30.3 %collective-permute-start.2 = (bf16[1,96,6,1,256]{4,1,3,2,0:T(8,128)(2,1)}, bf16[1,96,6,1,256]{4,1,3,2,0:T(8,128)(2,1)}, u32[]{:S(2)}, u32[]{:S(2)}) collective-permute-start(bf16[1,96,6,1,256]{4,1,3,2,0:T(8,128)(2,1)} %copy.97), channel_id=1, source_target_pairs={{0,1},{1,2},{2,3},{3,4},{4,5},{5,6},{6,7},{7,0},{8,9},{9,10},{10,1... | collective-permute-start | bytes 884744 | tf_op jit(solution)/shard_map/ppermute | solution.py:16
  63.0 8.3 %collective-permute-start.3 = (bf16[1,96,6,1,256]{4,1,3,2,0:T(8,128)(2,1)S(1)}, bf16[1,96,6,1,256]{4,1,3,2,0:T(8,128)(2,1)S(1)}, u32[]{:S(2)}, u32[]{:S(2)}) collective-permute-start(bf16[1,96,6,1,256]{4,1,3,2,0:T(8,128)(2,1)S(1)} %copy.98), channel_id=1, source_target_pairs={{1,0},{2,1},{3,2},{4,3},{5,4},{6,5},{7,6},{0,7},{9,8},{10,9},{11,1... | collective-permute-start | bytes 884744 | tf_op jit(solution)/shard_map/ppermute | solution.py:18
  89.7 3.2 copy-start.3
  89.7 3.2 copy-start.8
  111.6 1.6 copy-start.1
  116.2 90.3 %collective-permute-start.5 = (bf16[1,96,1,8,256]{4,3,2,1,0:T(8,128)(2,1)}, bf16[1,96,1,8,256]{4,3,2,1,0:T(8,128)(2,1)}, u32[]{:S(2)}, u32[]{:S(2)}) collective-permute-start(bf16[1,96,1,8,256]{4,3,2,1,0:T(8,128)(2,1)} %copy.73), channel_id=1, source_target_pairs={{8,0},{16,8},{24,16},{32,24},{40,32},{48,40},{56,48},{0,56},{9,1},... | collective-permute-start | bytes 1179656 | tf_op jit(solution)/shard_map/ppermute | solution.py:18
  117.4 90.6 %collective-permute-start.4 = (bf16[1,96,1,8,256]{4,3,2,1,0:T(8,128)(2,1)}, bf16[1,96,1,8,256]{4,3,2,1,0:T(8,128)(2,1)}, u32[]{:S(2)}, u32[]{:S(2)}) collective-permute-start(bf16[1,96,1,8,256]{4,3,2,1,0:T(8,128)(2,1)} %copy.72), channel_id=1, source_target_pairs={{0,8},{8,16},{16,24},{24,32},{32,40},{40,48},{48,56},{56,0},{1,9},... | collective-permute-start | bytes 1179656 | tf_op jit(solution)/shard_map/ppermute | solution.py:16
  135.8 63.2 %copy-start.2 = (bf16[4,8,8,33,96]{4,2,3,1,0:T(8,128)(2,1)S(1)}, bf16[4,8,8,33,96]{4,2,3,1,0:T(8,128)(2,1)}, u32[]{:S(2)}) copy-start(bf16[4,8,8,33,96]{4,2,3,1,0:T(8,128)(2,1)} %get-tuple-element.21) | copy-start | bytes 4866052
  210.3 1.6 copy-start
  211.9 6.1 %copy-start.6 = (f32[96]{0:T(128)S(1)}, f32[96]{0:T(128)}, u32[]{:S(2)}) copy-start(f32[96]{0:T(128)} %get-tuple-element.18) | copy-start | bytes 1156
  213.6 19.7 %collective-permute-start.7 = (bf16[1,96,6,1,256]{4,1,3,2,0:T(8,128)(2,1)S(1)}, bf16[1,96,6,1,256]{4,1,3,2,0:T(8,128)(2,1)S(1)}, u32[]{:S(2)}, u32[]{:S(2)}) collective-permute-start(bf16[1,96,6,1,256]{4,1,3,2,0:T(8,128)(2,1)S(1)} %copy.77), channel_id=1, source_target_pairs={{1,0},{2,1},{3,2},{4,3},{5,4},{6,5},{7,6},{0,7},{9,8},{10,9},{11,1... | collective-permute-start | bytes 884744 | tf_op jit(solution)/shard_map/ppermute | solution.py:18
  217.9 15.4 %collective-permute-start.6 = (bf16[1,96,6,1,256]{4,1,3,2,0:T(8,128)(2,1)S(1)}, bf16[1,96,6,1,256]{4,1,3,2,0:T(8,128)(2,1)S(1)}, u32[]{:S(2)}, u32[]{:S(2)}) collective-permute-start(bf16[1,96,6,1,256]{4,1,3,2,0:T(8,128)(2,1)S(1)} %copy.76), channel_id=1, source_target_pairs={{0,1},{1,2},{2,3},{3,4},{4,5},{5,6},{6,7},{7,0},{8,9},{9,10},{10,1... | collective-permute-start | bytes 884744 | tf_op jit(solution)/shard_map/ppermute | solution.py:16
  250.7 3.2 copy-start.4
  250.7 3.2 copy-start.9
Sparse Core Ops, SparseCore 0:
  206.6 25.3 reduce-scatter.3
where the time goes:
time: 537 us; the launch traced here: 531 us
  blocking collectives  283 us (53%)
  matrix products  96.9 us (18%)
  local copies, waits for them, and re-layouts  93.1 us (17%)
  waiting for transfers between devices  23.2 us (4%)
  between operations  16.1 us (3%)
  starting transfers between devices  11.3 us (2%)
  other arithmetic  6.9 us (1%)
    psum x1, blocking collectives, on_device(): lax.psum((group_part[0], group_part[1]), ('rad', 'azi'))  251 us
    transpose x1, matrix products, on_device(): kernel_grad.transpose(1, 2, 3, 4, 0).reshape(out_rows, 27 * channels)  63.2 us
    conv_general_dilated x2, matrix products, convolve(): lax.conv_general_dilated(left, right, (1, 1, 1), 'VALID', dimension_numbe...  33.7 us
    concatenate x3, local copies, waits for them, and re-layouts, rim_fix(): return jnp.concatenate([low_rim, extended[:, :, 1:-1], high_rim], axis=2)  27.2 us
    unnamed x32, local copies, waits for them, and re-layouts  25.5 us
    conv_general_dilated x6, local copies, waits for them, and re-layouts, convolve(): lax.conv_general_dilated(left, right, (1, 1, 1), 'VALID', dimension_numbe...  20.8 us
    unnamed x2, blocking collectives  20.1 us
    ppermute x4, waiting for transfers between devices, with_halo(): lax.ppermute(head, axis, [((i + 1) % count, i) for i in range(count)])  15.1 us
  transfers between devices with their start and end apart: 9, of which 3 were waited for; matrix products, arithmetic and copies ran while one was open for 28% of the time, Pallas kernels for 0%

commit v1 on v0

--- a/solution.py
+++ b/solution.py
@@ -90,7 +90,10 @@
             bias_term.astype(jnp.bfloat16), "dp", scatter_dimension=0, tiled=True
         ).astype(jnp.float32),
     )
-    weight_grad, bias_grad = lax.psum((group_part[0], group_part[1]), ("rad", "azi"))
+    guide_ends = lambda mat, shard_axis, ax_name: lax.psum(
+        lax.psum(mat, axis_name=shard_axis), axis_name=ax_name
+    )
+    weight_grad, bias_grad = guide_ends((group_part[0], group_part[1]), "rad", "azi")
     return (output, backward.astype(jnp.bfloat16), weight_grad, bias_grad)
 
 

time: 537 us -> 396 us (0.74)
  blocking collectives: 283 us -> 85.8 us
  waiting for transfers between devices: 23.2 us -> 75.1 us
    psum x1 -> x2, blocking collectives: 251 us -> 53 us  [the longest x1 38.3 us: on_device(): lax.psum(mat, axis_name=shard_axis)]
    psum x0 -> x1, waiting for transfers between devices: none -> 51.9 us  [on_device(): lax.psum(lax.psum(mat, axis_name=shard_axis), axis_name=ax_name)]
    unnamed x32 -> x33, local copies, waits for them, and re-layouts: 25.5 us -> 28.8 us
  transfers between devices with their start and end apart: 9 -> 10, of which waited for: 3 -> 4; matrix products, arithmetic and copies ran while one was open for 28% -> 38% of each run, Pallas kernels for 0% -> 0%
where the time goes in v1:
time: 396 us; the launch traced here: 390 us
  local copies, waits for them, and re-layouts  97.8 us (25%)
  matrix products  96.9 us (24%)
  blocking collectives  85.8 us (22%)
  waiting for transfers between devices  75.1 us (19%)
  between operations  16.2 us (4%)
  starting transfers between devices  11.3 us (3%)
  other arithmetic  6.91 us (2%)
    transpose x1, matrix products, on_device(): kernel_grad.transpose(1, 2, 3, 4, 0).reshape(out_rows, 27 * channels)  63.2 us
    psum x1, waiting for transfers between devices, on_device(): lax.psum(lax.psum(mat, axis_name=shard_axis), axis_name=ax_name)  51.9 us
    psum x1, blocking collectives, on_device(): lax.psum(mat, axis_name=shard_axis)  38.3 us
    conv_general_dilated x2, matrix products, convolve(): lax.conv_general_dilated(left, right, (1, 1, 1), 'VALID', dimension_numbe...  33.7 us
    unnamed x33, local copies, waits for them, and re-layouts  28.8 us
    concatenate x3, local copies, waits for them, and re-layouts, rim_fix(): return jnp.concatenate([low_rim, extended[:, :, 1:-1], high_rim], axis=2)  27.3 us
    conv_general_dilated x6, local copies, waits for them, and re-layouts, convolve(): lax.conv_general_dilated(left, right, (1, 1, 1), 'VALID', dimension_numbe...  20.8 us
    unnamed x2, blocking collectives  20.1 us
  transfers between devices with their start and end apart: 10, of which 4 were waited for; matrix products, arithmetic and copies ran while one was open for 38% of the time, Pallas kernels for 0%

profile of v1, /device:TPU:2, one launch (start us, length us, event | category | flops | bytes accessed | tf_op | source)
XLA Modules:
  0.0 390.1 jit_solution(7782347793337828013)
XLA Ops:
  7.2 1.2 fusion.42
  8.4 4.4 %collective-permute-start.1 = (bf16[1,96,1,8,256]{4,3,2,1,0:T(8,128)(2,1)S(1)}, bf16[1,96,1,8,256]{4,3,2,1,0:T(8,128)(2,1)S(1)}, u32[]{:S(2)}, u32[]{:S(2)}) collective-permute-start(bf16[1,96,1,8,256]{4,3,2,1,0:T(8,128)(2,1)S(1)} %get-tuple-element.36), channel_id=1, source_target_pairs={{8,0},{16,8},{24,16},{32,24},{40,32},{48,40},{56,48},{0,56},{9,1},... | collective-permute-start | bytes 1179656 | tf_op jit(solution)/shard_map/ppermute | solution.py:18
  12.8 9.5 %collective-permute-done.1 = bf16[1,96,1,8,256]{4,3,2,1,0:T(8,128)(2,1)S(1)} collective-permute-done((bf16[1,96,1,8,256]{4,3,2,1,0:T(8,128)(2,1)S(1)}, bf16[1,96,1,8,256]{4,3,2,1,0:T(8,128)(2,1)S(1)}, u32[]{:S(2)}, u32[]{:S(2)}) %collective-permute-start.1) | collective-permute-done | bytes 393248 | tf_op jit(solution)/shard_map/ppermute | solution.py:18
  22.3 8.0 %collective-permute-done = bf16[1,96,1,8,256]{4,3,2,1,0:T(8,128)(2,1)S(1)} collective-permute-done((bf16[1,96,1,8,256]{4,3,2,1,0:T(8,128)(2,1)S(1)}, bf16[1,96,1,8,256]{4,3,2,1,0:T(8,128)(2,1)S(1)}, u32[]{:S(2)}, u32[]{:S(2)}) %collective-permute-start) | collective-permute-done | bytes 393248 | tf_op jit(solution)/shard_map/ppermute | solution.py:16
  30.4 1.7 pad_maximum_fusion.3
  32.1 0.8 fusion.40
  32.9 0.8 copy.97
  33.6 0.6 fusion.43
  34.9 0.2 dynamic-update-slice
  35.1 8.6 %all-reduce = bf16[96]{0:T(256)(128)(2,1)S(1)} all-reduce(bf16[96]{0:T(256)(128)(2,1)S(1)} %dynamic-update-slice), channel_id=1, replica_groups=mesh['dp'=4,'rad'=8,'azi'=8] {'dp'}, use_global_device_ids=true, to_apply=%add | all-reduce | flops 96 | bytes 384
  43.8 12.8 %all_gather.6 = bf16[96,2592]{1,0:T(8,128)(2,1)S(1)} all-gather(bf16[24,2592]{1,0:T(8,128)(2,1)} %param.5), channel_id=1, replica_groups=mesh['dp'=4,'rad'=8,'azi'=8] {'dp'}, dimensions={0}, use_global_device_ids=true | all-gather | bytes 622080 | tf_op jit(solution)/shard_map/all_gather | solution.py:63
  56.6 1.1 copy.67
  57.7 4.6 %copy.69 = bf16[1,96,4,8,256]{1,3,4,2,0:T(8,128)(2,1)} copy(bf16[1,96,4,8,256]{4,3,2,1,0:T(8,128)(2,1)} %param.7) | data formatting | bytes 3145728 | tf_op args[3]
  63.0 0.9 collective-permute-start.3
  63.9 1.0 constant_dynamic-update-slice_fusion.2
  64.9 0.8 constant_dynamic-update-slice_fusion.1
  65.7 5.6 %collective-permute-done.3 = bf16[1,96,6,1,256]{4,1,3,2,0:T(8,128)(2,1)S(1)} collective-permute-done((bf16[1,96,6,1,256]{4,1,3,2,0:T(8,128)(2,1)S(1)}, bf16[1,96,6,1,256]{4,1,3,2,0:T(8,128)(2,1)S(1)}, u32[]{:S(2)}, u32[]{:S(2)}) %collective-permute-start.3) | collective-permute-done | bytes 294944 | tf_op jit(solution)/shard_map/ppermute | solution.py:18
  71.3 0.1 slice.65
  71.6 1.8 pad_maximum_fusion.1
  73.4 3.7 copy.88
  77.1 5.5 %pad.3.clone = bf16[96,6,10,1,264]{0,4,2,1,3:T(8,128)(2,1)} pad(bf16[96,6,10,1,256]{0,4,2,1,3:T(8,128)(2,1)} %copy.88, bf16[]{:T(256)} %constant.6.clone.1), padding=0_0x0_0x0_0x0_0x1_7 | pad | bytes 5990402 | tf_op jit(solution)/shard_map/concatenate | solution.py:32
  82.6 7.2 %reshape.21 = bf16[96,6,10,1,8,33]{0,5,4,2,1,3:T(8,128)(2,1)} reshape(bf16[96,6,10,1,264]{0,4,2,1,3:T(8,128)(2,1)} %pad.3.clone) | data formatting | bytes 6082560 | tf_op jit(solution)/shard_map/conv_general_dilated | solution.py:50
  89.8 3.1 copy.66
  93.0 18.0 %add_divide_fusion = (f32[4,8,8,33,96]{4,2,3,1,0:T(8,128)S(1)}, bf16[4,8,8,33,96]{4,2,3,1,0:T(8,128)(2,1)}, f32[4,8,8,33,96]{4,2,3,1,0:T(8,128)S(1)}) fusion(f32[96]{0:T(128)S(1)} %convert_element_type.36, pred[8,33]{0,1:T(8,128)(4,1)S(1)} %copy-done.8, bf16[96,3,3,3,96]{0,4,3,2,1:T(8,128)(2,1)S(1)} %bitcast.55, ...), kind=kOutput, calls=%fused_computation.6 | convolution fusion | flops 4222052352 | bytes 11810952 | tf_op jit(solution)/shard_map/conv_general_dilated | solution.py:50
  111.0 0.8 copy.71
  111.8 0.8 copy.70
  112.5 0.8 copy-done.1
  113.3 1.6 convert_reduce_fusion
  115.0 1.2 copy.73
  116.3 1.2 copy.72
  117.5 2.0 collective-permute-start.4
  119.5 16.4 %copy.83 = bf16[1,96,6,10,256]{1,0,4,3,2:T(2,128)(2,1)} copy(bf16[1,96,6,10,256]{4,1,3,2,0:T(8,128)(2,1)} %get-tuple-element.25) | data formatting | bytes 5898240 | tf_op jit(solution)/shard_map/concatenate | solution.py:32
  135.9 63.2 %fusion.28 = bf16[96,3,3,3,96]{0,4,3,2,1:T(8,128)(2,1)S(1)} fusion(bf16[1,96,6,10,256]{1,0,4,3,2:T(2,128)(2,1)} %copy.83, bf16[1,96,4,8,256]{1,3,4,2,0:T(8,128)(2,1)S(1)} %get-tuple-element.19), kind=kOutput, calls=%fused_computation.38 | convolution fusion | flops 4066744320 | bytes 5019648 | tf_op jit(solution)/shard_map/transpose | solution.py:82
  199.1 0.3 copy.68
  199.4 1.5 slice_bitcast_fusion.3
  200.9 4.6 %copy.86 = bf16[1,96,4,8,256]{4,3,2,1,0:T(8,128)(2,1)} copy(bf16[1,96,4,8,256]{1,3,4,2,0:T(8,128)(2,1)} %slice_bitcast_fusion.3) | data formatting | bytes 3145728
  205.5 1.1 copy.85
  206.7 1.5 copy.75
  208.2 1.5 copy.74
  209.7 0.7 pad_maximum_fusion
  210.5 1.6 copy-done
  212.1 1.2 fusion.39
  213.3 0.5 copy.77
  213.8 3.8 collective-permute-start.7
  217.6 0.5 copy.76
  218.1 0.1 collective-permute-start.6
  218.2 11.4 %all-reduce.2 = bf16[96]{0:T(256)(128)(2,1)S(1)} all-reduce(bf16[96]{0:T(256)(128)(2,1)S(1)} %multiply_convert_fusion.1), channel_id=3, replica_groups=mesh['dp'=4,'rad'=8,'azi'=8] {'dp'}, use_global_device_ids=true, to_apply=%region_4.5.clone | all-reduce | flops 96 | bytes 384
  229.7 3.7 copy.78
  233.5 0.4 pad_maximum_fusion.2
  233.8 0.1 slice.75
  234.0 0.1 maximum_select_fusion.1
  234.1 0.4 maximum_bitcast_fusion
  234.5 3.7 copy.89
  238.2 5.4 %pad.5.clone = bf16[96,6,10,1,264]{0,4,2,1,3:T(8,128)(2,1)} pad(bf16[96,6,10,1,256]{0,4,2,1,3:T(8,128)(2,1)} %copy.89, bf16[]{:T(256)} %constant.6.clone.1), padding=0_0x0_0x0_0x0_0x1_7 | pad | bytes 5990402 | tf_op jit(solution)/shard_map/concatenate | solution.py:32
  243.6 7.2 %reshape.28 = bf16[96,6,10,1,8,33]{0,5,4,2,1,3:T(8,128)(2,1)} reshape(bf16[96,6,10,1,264]{0,4,2,1,3:T(8,128)(2,1)} %pad.5.clone) | data formatting | bytes 6082560 | tf_op jit(solution)/shard_map/conv_general_dilated | solution.py:50
  250.8 3.1 copy.81
  254.0 15.8 %select_convert_fusion = bf16[4,8,8,33,96]{4,2,3,1,0:T(8,128)(2,1)S(1)} fusion(pred[8,33]{0,1:T(8,128)(4,1)S(1)} %copy-done.9, bf16[96,3,3,3,96]{0,4,3,2,1:T(8,128)(2,1)S(1)} %bitcast.56, bf16[96,6,10,1,7,2]{0,4,5,2,1,3:T(8,128)(2,1)S(1)} %slice.76, bf16[96,6,10,1,8,33]{0,4,5,2,1,3:T(8,128)(2,1)S(1)} %copy.81), kind=kOutput, calls=%fused_computation.3 | convolution fusion | flops 4215564288 | bytes 5322504 | tf_op jit(solution)/shard_map/conv_general_dilated | solution.py:50
  269.8 0.3 copy.82
  270.1 38.3 %all-reduce.8 = (f32[24,2592]{1,0:T(8,128)}, f32[24]{0:T(128)S(1)}) all-reduce(bf16[24,2592]{1,0:T(8,128)(2,1)} %reduce-scatter.4.cloned.1.call-done, f32[24]{0:T(128)S(1)} %dynamic-slice_convert_fusion), channel_id=1, replica_groups=mesh['dp'=4,'rad'=8,'azi'=8] {'rad'}, use_global_device_ids=true, to_apply=%region_1.2 | all-reduce | flops 62232 | bytes 373440 | tf_op jit(solution)/shard_map/psum | solution.py:94
  308.4 1.5 slice_bitcast_fusion.2
  309.9 4.6 %copy.87 = bf16[1,96,4,8,256]{4,3,2,1,0:T(8,128)(2,1)} copy(bf16[1,96,4,8,256]{1,3,4,2,0:T(8,128)(2,1)} %slice_bitcast_fusion.2) | data formatting | bytes 3145728
  314.6 14.7 %psum.31 = f32[24]{0:T(128)} all-reduce(f32[24]{0:T(128)S(1)} %get-tuple-element.17), channel_id=1, replica_groups=mesh['dp'=4,'rad'=8,'azi'=8] {'azi'}, use_global_device_ids=true, to_apply=%region_6.7 | all-reduce | flops 24 | bytes 192 | tf_op jit(solution)/shard_map/psum | solution.py:93
  329.3 51.9 %all-reduce.7.cloned.1.call-done = f32[24,2592]{1,0:T(8,128)} async-done(((f32[24,2592]{1,0:T(8,128)}), f32[24,2592]{1,0:T(8,128)}) %all-reduce.7.cloned.1.call-update) | async-done | bytes 248848 | tf_op jit(solution)/shard_map/psum | solution.py:93
  381.1 1.7 copy.106
  (41 shorter events, 0.6 us)
Async XLA Ops:
  7.2 263.0 %reduce-scatter.4.cloned.1.call-start = ((), (), s32[]{:S(2)}) async-start(), calls=%async_computation.2 | async-start | bytes 645120
  8.4 13.9 %collective-permute-start.1 = (bf16[1,96,1,8,256]{4,3,2,1,0:T(8,128)(2,1)S(1)}, bf16[1,96,1,8,256]{4,3,2,1,0:T(8,128)(2,1)S(1)}, u32[]{:S(2)}, u32[]{:S(2)}) collective-permute-start(bf16[1,96,1,8,256]{4,3,2,1,0:T(8,128)(2,1)S(1)} %get-tuple-element.36), channel_id=1, source_target_pairs={{8,0},{16,8},{24,16},{32,24},{40,32},{48,40},{56,48},{0,56},{9,1},... | collective-permute-start | bytes 1179656 | tf_op jit(solution)/shard_map/ppermute | solution.py:18
  12.8 20.8 %copy-start.5 = (u32[256]{0:T(256)S(1)}, u32[256]{0:T(256)}, u32[]{:S(2)}) copy-start(u32[256]{0:T(256)} %constant.33) | copy-start | bytes 3076
  12.8 22.0 %copy-start.7 = (bf16[24]{0:T(256)(128)(2,1)S(1)}, bf16[24]{0:T(256)(128)(2,1)}, u32[]{:S(2)}) copy-start(bf16[24]{0:T(256)(128)(2,1)} %param.6) | copy-start | bytes 148
  12.8 17.5 %collective-permute-start = (bf16[1,96,1,8,256]{4,3,2,1,0:T(8,128)(2,1)S(1)}, bf16[1,96,1,8,256]{4,3,2,1,0:T(8,128)(2,1)S(1)}, u32[]{:S(2)}, u32[]{:S(2)}) collective-permute-start(bf16[1,96,1,8,256]{4,3,2,1,0:T(8,128)(2,1)S(1)} %get-tuple-element.35), channel_id=1, source_target_pairs={{0,8},{8,16},{16,24},{24,32},{32,40},{40,48},{48,56},{56,0},{1,9},... | collective-permute-start | bytes 1179656 | tf_op jit(solution)/shard_map/ppermute | solution.py:16
  33.6 30.3 %collective-permute-start.2 = (bf16[1,96,6,1,256]{4,1,3,2,0:T(8,128)(2,1)}, bf16[1,96,6,1,256]{4,1,3,2,0:T(8,128)(2,1)}, u32[]{:S(2)}, u32[]{:S(2)}) collective-permute-start(bf16[1,96,6,1,256]{4,1,3,2,0:T(8,128)(2,1)} %copy.97), channel_id=1, source_target_pairs={{0,1},{1,2},{2,3},{3,4},{4,5},{5,6},{6,7},{7,0},{8,9},{9,10},{10,1... | collective-permute-start | bytes 884744 | tf_op jit(solution)/shard_map/ppermute | solution.py:16
  63.0 8.3 %collective-permute-start.3 = (bf16[1,96,6,1,256]{4,1,3,2,0:T(8,128)(2,1)S(1)}, bf16[1,96,6,1,256]{4,1,3,2,0:T(8,128)(2,1)S(1)}, u32[]{:S(2)}, u32[]{:S(2)}) collective-permute-start(bf16[1,96,6,1,256]{4,1,3,2,0:T(8,128)(2,1)S(1)} %copy.98), channel_id=1, source_target_pairs={{1,0},{2,1},{3,2},{4,3},{5,4},{6,5},{7,6},{0,7},{9,8},{10,9},{11,1... | collective-permute-start | bytes 884744 | tf_op jit(solution)/shard_map/ppermute | solution.py:18
  89.8 3.2 copy-start.3
  89.8 3.2 copy-start.8
  111.7 1.6 copy-start.1
  116.3 90.4 %collective-permute-start.5 = (bf16[1,96,1,8,256]{4,3,2,1,0:T(8,128)(2,1)}, bf16[1,96,1,8,256]{4,3,2,1,0:T(8,128)(2,1)}, u32[]{:S(2)}, u32[]{:S(2)}) collective-permute-start(bf16[1,96,1,8,256]{4,3,2,1,0:T(8,128)(2,1)} %copy.73), channel_id=1, source_target_pairs={{8,0},{16,8},{24,16},{32,24},{40,32},{48,40},{56,48},{0,56},{9,1},... | collective-permute-start | bytes 1179656 | tf_op jit(solution)/shard_map/ppermute | solution.py:18
  117.5 90.7 %collective-permute-start.4 = (bf16[1,96,1,8,256]{4,3,2,1,0:T(8,128)(2,1)}, bf16[1,96,1,8,256]{4,3,2,1,0:T(8,128)(2,1)}, u32[]{:S(2)}, u32[]{:S(2)}) collective-permute-start(bf16[1,96,1,8,256]{4,3,2,1,0:T(8,128)(2,1)} %copy.72), channel_id=1, source_target_pairs={{0,8},{8,16},{16,24},{24,32},{32,40},{40,48},{48,56},{56,0},{1,9},... | collective-permute-start | bytes 1179656 | tf_op jit(solution)/shard_map/ppermute | solution.py:16
  135.9 63.2 %copy-start.2 = (bf16[4,8,8,33,96]{4,2,3,1,0:T(8,128)(2,1)S(1)}, bf16[4,8,8,33,96]{4,2,3,1,0:T(8,128)(2,1)}, u32[]{:S(2)}) copy-start(bf16[4,8,8,33,96]{4,2,3,1,0:T(8,128)(2,1)} %get-tuple-element.21) | copy-start | bytes 4866052
  206.6 174.5 %all-reduce.7.cloned.1.call-start = ((), (), s32[]{:S(2)}) async-start(), calls=%async_computation.1 | async-start | bytes 516096 | tf_op jit(solution)/shard_map/psum | solution.py:93
  210.5 1.6 copy-start
  212.1 6.1 %copy-start.6 = (f32[96]{0:T(128)S(1)}, f32[96]{0:T(128)}, u32[]{:S(2)}) copy-start(f32[96]{0:T(128)} %get-tuple-element.18) | copy-start | bytes 1156
  213.8 19.7 %collective-permute-start.7 = (bf16[1,96,6,1,256]{4,1,3,2,0:T(8,128)(2,1)S(1)}, bf16[1,96,6,1,256]{4,1,3,2,0:T(8,128)(2,1)S(1)}, u32[]{:S(2)}, u32[]{:S(2)}) collective-permute-start(bf16[1,96,6,1,256]{4,1,3,2,0:T(8,128)(2,1)S(1)} %copy.77), channel_id=1, source_target_pairs={{1,0},{2,1},{3,2},{4,3},{5,4},{6,5},{7,6},{0,7},{9,8},{10,9},{11,1... | collective-permute-start | bytes 884744 | tf_op jit(solution)/shard_map/ppermute | solution.py:18
  218.1 15.4 %collective-permute-start.6 = (bf16[1,96,6,1,256]{4,1,3,2,0:T(8,128)(2,1)S(1)}, bf16[1,96,6,1,256]{4,1,3,2,0:T(8,128)(2,1)S(1)}, u32[]{:S(2)}, u32[]{:S(2)}) collective-permute-start(bf16[1,96,6,1,256]{4,1,3,2,0:T(8,128)(2,1)S(1)} %copy.76), channel_id=1, source_target_pairs={{0,1},{1,2},{2,3},{3,4},{4,5},{5,6},{6,7},{7,0},{8,9},{9,10},{10,1... | collective-permute-start | bytes 884744 | tf_op jit(solution)/shard_map/ppermute | solution.py:16
  250.8 3.2 copy-start.4
  250.8 3.2 copy-start.9
Sparse Core Ops, SparseCore 0:
  206.7 25.3 reduce-scatter.3
  308.6 72.5 all-reduce.6
